TPU v7x, 256 devices: a whole 4x4x8 slice. The times are simulated.
256 devices in a mesh: lat: 4 (over x_lo, core), lon: 64 (over x_hi, y, z).
Axes of the slice: x: 4 (x_hi: 2, x_lo: 2; x = x_hi * 2 + x_lo), y: 4, z: 8, core: 2. Of those that a mesh axis runs over, the one named last changes fastest.
Arguments:
- queries: bfloat16 [64, 1024, 1536], P('lat', 'lon'), may hold values from -12 to 12
- key_tokens: bfloat16 [64, 1024, 1536], P('lat', 'lon'), may hold values from -4 to 4
- value_tokens: bfloat16 [64, 1024, 1536], P('lat', 'lon'), may hold values from -6 to 6
- block_lists: int32 [8, 64, 8], P('lat', 'lon'), may hold values from 0 to 9, as said below
- band_rows: int32 [4, 1024], P('lat', 'lon'), may hold values from 0 to 255, as said below
Outputs:
- attended: bfloat16 [64, 1024, 1536], P('lat', 'lon')
Inputs may be any that keep to these rules, and one draw needn't show every extreme that they name: `block_lists`: entry 0 of the list of query block b of a tile is its own block, 4 + b; the other entries are distinct candidate numbers, also distinct from entry 0. `band_rows`: the 16 token numbers of each tile are distinct.
All inputs are finite; a program needn't handle non-finite values.
Results may differ from a plain program's by a relative error of at most 0.0047.
Values may be sent and summed in bfloat16 or wider, within the bound.
No kernel may reach another device: no remote copies, remote signals or barrier semaphores. Data moves between devices by JAX's collectives and lax.ppermute only.
A program may use at most 128 MiB of HBM per device.

v0:
```python
import jax
import jax.numpy as jnp
from jax import lax
from jax.sharding import PartitionSpec as P

H = 24
HD = 64
BR = 8
BW = 16


def from_behind(value, axis, steps):
    count = lax.axis_size(axis)
    pairs = [(source, (source + steps) % count) for source in range(count)]
    return lax.ppermute(value, axis, pairs)


def block_attention(q_rows, key_set, value_set, live_mask):
    count = q_rows.shape[0]
    q_heads = q_rows.reshape(count, H, HD)
    k_heads = key_set.reshape(key_set.shape[0], H, HD)
    v_heads = value_set.reshape(value_set.shape[0], H, HD)
    scores = jnp.einsum(
        "qhd,khd->hqk", q_heads, k_heads, preferred_element_type=jnp.float32
    ) * HD ** (-0.5)
    scores = jnp.where(live_mask[None, None, :], scores, -jnp.inf)
    row_max = jnp.max(scores, axis=-1, keepdims=True)
    exp_scores = jnp.exp(scores - row_max)
    totals = jnp.sum(exp_scores, axis=-1)
    weights = exp_scores.astype(jnp.bfloat16)
    mixture = jnp.einsum("hqk,khd->qhd", weights, v_heads, preferred_element_type=jnp.float32)
    mixture = mixture / jnp.transpose(totals)[:, :, None]
    return mixture.reshape(count, H * HD).astype(jnp.bfloat16)


def local(queries, key_tokens, value_tokens, block_lists, band_rows):
    tile_lat, tile_lon, feature = queries.shape
    block_len = BR * BW
    tile_blocks = tile_lat // BR
    lat_size = lax.axis_size("lat")
    west_two = from_behind((key_tokens, value_tokens), "lon", 2)
    west_one = from_behind((key_tokens, value_tokens), "lon", 1)
    east_one = from_behind((key_tokens, value_tokens), "lon", -1)
    east_two = from_behind((key_tokens, value_tokens), "lon", -2)
    sources = (west_two, west_one, (key_tokens, value_tokens), east_one, east_two)
    cand_keys = jnp.concatenate(
        [entry[0].reshape(tile_blocks, block_len, feature) for entry in sources], 0
    )
    cand_values = jnp.concatenate(
        [entry[1].reshape(tile_blocks, block_len, feature) for entry in sources], 0
    )
    picked_keys = key_tokens.reshape(tile_lat * tile_lon, feature)[band_rows[0]]
    picked_values = value_tokens.reshape(tile_lat * tile_lon, feature)[band_rows[0]]
    band_keys, band_values = (
        lax.all_gather(picked_keys, "lon", axis=0, tiled=True),
        lax.all_gather(picked_values, "lon", axis=0, tiled=True),
    )
    lat_at = lax.axis_index("lat")
    is_polar = (lat_at == 0) | (lat_at == lat_size - 1)
    listed_all = block_lists[:, 0, :]
    band_live = jnp.ones((band_keys.shape[0],), jnp.bool_)
    query_blocks = queries.reshape(tile_blocks, block_len, feature)

    def one_block(inputs):
        q_rows, listed = inputs
        near_keys = cand_keys[listed].reshape(-1, feature)
        near_values = cand_values[listed].reshape(-1, feature)
        near_live = jnp.ones((near_keys.shape[0],), jnp.bool_)

        def with_band():
            key_set = jnp.concatenate([near_keys, band_keys], 0)
            value_set = jnp.concatenate([near_values, band_values], 0)
            live_mask = jnp.concatenate([near_live, band_live], 0)
            return block_attention(q_rows, key_set, value_set, live_mask)

        def near_only():
            return block_attention(q_rows, near_keys, near_values, near_live)

        return lax.cond(is_polar, with_band, near_only)

    results = lax.map(one_block, (query_blocks, listed_all))
    return results.reshape(tile_lat, tile_lon, feature)


def solution(mesh):
    return jax.shard_map(
        local,
        mesh=mesh,
        in_specs=(
            P("lat", "lon", None),
            P("lat", "lon", None),
            P("lat", "lon", None),
            P("lat", "lon", None),
            P("lat", "lon"),
        ),
        out_specs=P("lat", "lon", None),
        check_vma=False,
    )
```

profile of v0, /device:TPU:8, one launch (start us, length us, event | category | flops | bytes accessed | tf_op | source)
XLA Modules:
  0.0 465.4 jit_solution(9054206073713176776)
XLA Ops:
  12.4 3.3 collective-permute-start.4
  15.8 4.5 collective-permute-start
  24.4 20.5 %collective-permute-done.4 = bf16[16,16,1536]{2,1,0:T(8,128)(2,1)} collective-permute-done((bf16[16,16,1536]{2,1,0:T(8,128)(2,1)}, bf16[16,16,1536]{2,1,0:T(8,128)(2,1)}, u32[]{:S(2)}, u32[]{:S(2)}) %collective-permute-start.4) | collective-permute-done | bytes 786464 | tf_op jit(solution)/shard_map/ppermute | solution.py:15
  44.9 28.6 %collective-permute-start.6 = (bf16[16,16,1536]{2,1,0:T(8,128)(2,1)}, bf16[16,16,1536]{2,1,0:T(8,128)(2,1)S(1)}, u32[]{:S(2)}, u32[]{:S(2)}) collective-permute-start(bf16[16,16,1536]{2,1,0:T(8,128)(2,1)} %param.11), channel_id=1, source_target_pairs={{0,63},{1,0},{2,1},{3,2},{4,3},{5,4},{6,5},{7,6},{8,7},{9,8},{10,9... | collective-permute-start | bytes 2359304 | tf_op jit(solution)/shard_map/ppermute | solution.py:15
  75.6 5.3 %collective-permute-done = bf16[16,16,1536]{2,1,0:T(8,128)(2,1)} collective-permute-done((bf16[16,16,1536]{2,1,0:T(8,128)(2,1)}, bf16[16,16,1536]{2,1,0:T(8,128)(2,1)}, u32[]{:S(2)}, u32[]{:S(2)}) %collective-permute-start) | collective-permute-done | bytes 786464 | tf_op jit(solution)/shard_map/ppermute | solution.py:15
  80.9 12.4 %collective-permute-start.7 = (bf16[16,16,1536]{2,1,0:T(8,128)(2,1)}, bf16[16,16,1536]{2,1,0:T(8,128)(2,1)S(1)}, u32[]{:S(2)}, u32[]{:S(2)}) collective-permute-start(bf16[16,16,1536]{2,1,0:T(8,128)(2,1)} %param.11), channel_id=1, source_target_pairs={{0,62},{1,63},{2,0},{3,1},{4,2},{5,3},{6,4},{7,5},{8,6},{9,7},{10,... | collective-permute-start | bytes 2359304 | tf_op jit(solution)/shard_map/ppermute | solution.py:15
  95.5 12.5 %collective-permute-done.5 = bf16[16,16,1536]{2,1,0:T(8,128)(2,1)} collective-permute-done((bf16[16,16,1536]{2,1,0:T(8,128)(2,1)}, bf16[16,16,1536]{2,1,0:T(8,128)(2,1)}, u32[]{:S(2)}, u32[]{:S(2)}) %collective-permute-start.5) | collective-permute-done | bytes 786464 | tf_op jit(solution)/shard_map/ppermute | solution.py:15
  114.8 33.9 %collective-permute-done.7 = bf16[16,16,1536]{2,1,0:T(8,128)(2,1)S(1)} collective-permute-done((bf16[16,16,1536]{2,1,0:T(8,128)(2,1)}, bf16[16,16,1536]{2,1,0:T(8,128)(2,1)S(1)}, u32[]{:S(2)}, u32[]{:S(2)}) %collective-permute-start.7) | collective-permute-done | bytes 786464 | tf_op jit(solution)/shard_map/ppermute | solution.py:15
  152.5 14.9 %collective-permute-done.3 = bf16[16,16,1536]{2,1,0:T(8,128)(2,1)S(1)} collective-permute-done((bf16[16,16,1536]{2,1,0:T(8,128)(2,1)S(1)}, bf16[16,16,1536]{2,1,0:T(8,128)(2,1)S(1)}, u32[]{:S(2)}, u32[]{:S(2)}) %collective-permute-start.3) | collective-permute-done | bytes 786464 | tf_op jit(solution)/shard_map/ppermute | solution.py:15
  168.3 26.5 %all-gather.7.cloned.1.call-done = bf16[1024,1536]{1,0:T(8,128)(2,1)} async-done(((bf16[16,1536]{1,0:T(8,128)(2,1)}), bf16[1024,1536]{1,0:T(8,128)(2,1)}) %all-gather.7.cloned.1.call-update) | async-done | bytes 3145744 | tf_op jit(solution)/shard_map/all_gather | solution.py:55
  194.8 4.7 %copy.17 = bf16[1024,1536]{0,1:T(8,128)(2,1)} copy(bf16[1024,1536]{1,0:T(8,128)(2,1)} %all-gather.7.cloned.1.call-done) | data formatting | bytes 6291456 | tf_op jit(solution)/shard_map/while | solution.py:81
  199.5 121.2 %all-gather.5.cloned.1.call-done = bf16[1024,1536]{1,0:T(8,128)(2,1)} async-done(((bf16[16,1536]{1,0:T(8,128)(2,1)}), bf16[1024,1536]{1,0:T(8,128)(2,1)}) %all-gather.5.cloned.1.call-update) | async-done | bytes 3145744 | tf_op jit(solution)/shard_map/all_gather | solution.py:56
  320.7 4.6 copy.16
  325.4 133.2 %while.10 = (s32[]{:T(128)}, bf16[2,128,1536]{2,1,0:T(8,128)(2,1)}, pred[]{:T(512)}, bf16[2,128,1536]{2,1,0:T(8,128)(2,1)}, s32[2,8]{1,0:T(2,128)S(1)}, /*index=...) while((s32[]{:T(128)}, bf16[2,128,1536]{2,1,0:T(8,128)(2,1)}, ...), condition=%wide.region_7.8_spmd, body=%wide.region_0.7_spmd.sunk | while | flops 1686498304 | bytes 169148896 | solution.py:81
  329.5 4.5 gather_fusion
  334.1 55.2 %conditional.7 = (bf16[1,128,1536]{1,2,0:T(8,128)(2,1)S(1)}) conditional(s32[]{:T(128)} %convert_element_type.36, (bf16[128,1536]{0,1:T(8,128)(2,1)S(1)}, bf16[8,128,1536]{2,1,0:T(8,128)(2,1)}, bf16[8,128,1536]{2,1,0:T(8,128)(2,1)S(1)}) %tuple.53, (bf16[8,128,1536]{2,1,0:T(8,128)(2,1)S(1)}, bf16[1024,1536]{0,1:T(8,128)(2,1)}, ...), branch_computations={%region_1.3_spmd, %region_4.6_spmd} | conditional | flops 1686497280 | bytes 151842912
  334.1 5.0 %copy.14 = bf16[8,128,1536]{1,0,2:T(8,128)(2,1)} copy(bf16[8,128,1536]{2,1,0:T(8,128)(2,1)} %get-tuple-element.102) | data formatting | bytes 6291456 | tf_op jit(solution)/shard_map
  339.1 5.8 %concatenate.17 = bf16[1024,24,64]{0,2,1:T(8,128)(2,1)} reshape(bf16[8,128,1536]{1,0,2:T(8,128)(2,1)} %copy.14) | data formatting | bytes 6291456 | tf_op jit(solution)/shard_map/while/body/eval_jaxpr/cond/branch_1_fun/concatenate | solution.py:71
  344.9 3.4 copy.13
  348.3 6.0 %concatenate.2 = bf16[1024,24,64]{0,2,1:T(8,128)(2,1)} reshape(bf16[8,128,1536]{1,0,2:T(8,128)(2,1)} %copy.13) | data formatting | bytes 6291456 | tf_op jit(solution)/shard_map/while/body/eval_jaxpr/cond/branch_1_fun/concatenate | solution.py:72
  354.2 11.8 %bitcast_reduce_fusion = (f32[24,128]{1,0:T(8,128)S(1)}, f32[24,2048,128]{2,1,0:T(8,128)}) fusion(bf16[128,24,64]{0,2,1:T(8,128)(2,1)S(1)} %bitcast.100, bf16[1024,24,64]{0,2,1:T(8,128)(2,1)} %bitcast.96, bf16[1024,24,64]{0,2,1:T(8,128)(2,1)S(1)} %copy-done.2), kind=kOutput, calls=%fused_computation.15 | convolution fusion | flops 830469120 | bytes 31862784 | tf_op jit(solution)/shard_map/while/body/eval_jaxpr/cond/branch_1_fun/qhd,khd->hqk/dot_general | solution.py:23
  366.1 11.7 %fusion.14 = f32[24,128]{1,0:T(8,128)S(1)} fusion(f32[24,2048,128]{2,1,0:T(8,128)} %get-tuple-element.135, f32[24,128]{1,0:T(8,128)S(1)} %get-tuple-element.134), kind=kLoop, calls=%fused_computation.17 | loop fusion | flops 18871296 | bytes 25190400 | tf_op jit(solution)/shard_map/while/body/eval_jaxpr/cond/branch_1_fun/reduce_sum | solution.py:29
  377.8 11.5 %fusion.32 = bf16[128,24,64]{0,2,1:T(8,128)(2,1)S(1)} fusion(f32[24,2048,128]{2,1,0:T(8,128)} %get-tuple-element.135, f32[24,128]{1,0:T(8,128)S(1)} %get-tuple-element.134, bf16[1024,24,64]{0,2,1:T(8,128)(2,1)S(1)} %bitcast.103, bf16[1024,24,64]{0,2,1:T(8,128)(2,1)S(1)} %copy-done.4, f32[128,24]{0,1:T(8,128)S(1)} %bitcast.113), kind=kOutput, calls=%fused_computation.30 | convolution fusion | flops 837156864 | bytes 31875072 | tf_op jit(solution)/shard_map/while/body/eval_jaxpr/cond/branch_1_fun/hqk,khd->qhd/dot_general | solution.py:31
  396.1 4.5 gather_fusion
  400.7 55.2 %conditional.7 = (bf16[1,128,1536]{1,2,0:T(8,128)(2,1)S(1)}) conditional(s32[]{:T(128)} %convert_element_type.36, (bf16[128,1536]{0,1:T(8,128)(2,1)S(1)}, bf16[8,128,1536]{2,1,0:T(8,128)(2,1)}, bf16[8,128,1536]{2,1,0:T(8,128)(2,1)S(1)}) %tuple.53, (bf16[8,128,1536]{2,1,0:T(8,128)(2,1)S(1)}, bf16[1024,1536]{0,1:T(8,128)(2,1)}, ...), branch_computations={%region_1.3_spmd, %region_4.6_spmd} | conditional | flops 1686497280 | bytes 151842912
  400.7 5.0 %copy.14 = bf16[8,128,1536]{1,0,2:T(8,128)(2,1)} copy(bf16[8,128,1536]{2,1,0:T(8,128)(2,1)} %get-tuple-element.102) | data formatting | bytes 6291456 | tf_op jit(solution)/shard_map
  405.7 5.8 %concatenate.17 = bf16[1024,24,64]{0,2,1:T(8,128)(2,1)} reshape(bf16[8,128,1536]{1,0,2:T(8,128)(2,1)} %copy.14) | data formatting | bytes 6291456 | tf_op jit(solution)/shard_map/while/body/eval_jaxpr/cond/branch_1_fun/concatenate | solution.py:71
  411.5 3.4 copy.13
  414.9 6.0 %concatenate.2 = bf16[1024,24,64]{0,2,1:T(8,128)(2,1)} reshape(bf16[8,128,1536]{1,0,2:T(8,128)(2,1)} %copy.13) | data formatting | bytes 6291456 | tf_op jit(solution)/shard_map/while/body/eval_jaxpr/cond/branch_1_fun/concatenate | solution.py:72
  420.8 11.8 %bitcast_reduce_fusion = (f32[24,128]{1,0:T(8,128)S(1)}, f32[24,2048,128]{2,1,0:T(8,128)}) fusion(bf16[128,24,64]{0,2,1:T(8,128)(2,1)S(1)} %bitcast.100, bf16[1024,24,64]{0,2,1:T(8,128)(2,1)} %bitcast.96, bf16[1024,24,64]{0,2,1:T(8,128)(2,1)S(1)} %copy-done.2), kind=kOutput, calls=%fused_computation.15 | convolution fusion | flops 830469120 | bytes 31862784 | tf_op jit(solution)/shard_map/while/body/eval_jaxpr/cond/branch_1_fun/qhd,khd->hqk/dot_general | solution.py:23
  432.7 11.7 %fusion.14 = f32[24,128]{1,0:T(8,128)S(1)} fusion(f32[24,2048,128]{2,1,0:T(8,128)} %get-tuple-element.135, f32[24,128]{1,0:T(8,128)S(1)} %get-tuple-element.134), kind=kLoop, calls=%fused_computation.17 | loop fusion | flops 18871296 | bytes 25190400 | tf_op jit(solution)/shard_map/while/body/eval_jaxpr/cond/branch_1_fun/reduce_sum | solution.py:29
  444.4 11.5 %fusion.32 = bf16[128,24,64]{0,2,1:T(8,128)(2,1)S(1)} fusion(f32[24,2048,128]{2,1,0:T(8,128)} %get-tuple-element.135, f32[24,128]{1,0:T(8,128)S(1)} %get-tuple-element.134, bf16[1024,24,64]{0,2,1:T(8,128)(2,1)S(1)} %bitcast.103, bf16[1024,24,64]{0,2,1:T(8,128)(2,1)S(1)} %copy-done.4, f32[128,24]{0,1:T(8,128)S(1)} %bitcast.113), kind=kOutput, calls=%fused_computation.30 | convolution fusion | flops 837156864 | bytes 31875072 | tf_op jit(solution)/shard_map/while/body/eval_jaxpr/cond/branch_1_fun/hqk,khd->qhd/dot_general | solution.py:31
  (62 shorter events, 39.4 us)
Async XLA Ops:
  6.5 101.5 %copy-start.8 = (bf16[16,16,1536]{2,1,0:T(8,128)(2,1)S(1)}, bf16[16,16,1536]{2,1,0:T(8,128)(2,1)}, u32[]{:S(2)}) copy-start(bf16[16,16,1536]{2,1,0:T(8,128)(2,1)} %param.10) | copy-start | bytes 2359300
  6.5 106.4 %copy-start.7 = (bf16[16,16,1536]{2,1,0:T(8,128)(2,1)S(1)}, bf16[16,16,1536]{2,1,0:T(8,128)(2,1)}, u32[]{:S(2)}) copy-start(bf16[16,16,1536]{2,1,0:T(8,128)(2,1)} %param.11) | copy-start | bytes 2359300
  6.5 188.3 %all-gather.7.cloned.1.call-start = ((), (), s32[]{:S(2)}) async-start(), calls=%async_computation.1 | async-start | bytes 3194880 | tf_op jit(solution)/shard_map/all_gather | solution.py:55
  9.8 310.9 %all-gather.5.cloned.1.call-start = ((), (), s32[]{:S(2)}) async-start(), calls=%async_computation | async-start | bytes 3194880 | tf_op jit(solution)/shard_map/all_gather | solution.py:56
  12.4 32.5 %collective-permute-start.4 = (bf16[16,16,1536]{2,1,0:T(8,128)(2,1)}, bf16[16,16,1536]{2,1,0:T(8,128)(2,1)}, u32[]{:S(2)}, u32[]{:S(2)}) collective-permute-start(bf16[16,16,1536]{2,1,0:T(8,128)(2,1)} %param.11), channel_id=1, source_target_pairs={{0,2},{1,3},{2,4},{3,5},{4,6},{5,7},{6,8},{7,9},{8,10},{9,11},{10,... | collective-permute-start | bytes 2359304 | tf_op jit(solution)/shard_map/ppermute | solution.py:15
  15.8 65.2 %collective-permute-start = (bf16[16,16,1536]{2,1,0:T(8,128)(2,1)}, bf16[16,16,1536]{2,1,0:T(8,128)(2,1)}, u32[]{:S(2)}, u32[]{:S(2)}) collective-permute-start(bf16[16,16,1536]{2,1,0:T(8,128)(2,1)} %param.10), channel_id=1, source_target_pairs={{0,2},{1,3},{2,4},{3,5},{4,6},{5,7},{6,8},{7,9},{8,10},{9,11},{10,... | collective-permute-start | bytes 2359304 | tf_op jit(solution)/shard_map/ppermute | solution.py:15
  20.2 87.8 %collective-permute-start.5 = (bf16[16,16,1536]{2,1,0:T(8,128)(2,1)}, bf16[16,16,1536]{2,1,0:T(8,128)(2,1)}, u32[]{:S(2)}, u32[]{:S(2)}) collective-permute-start(bf16[16,16,1536]{2,1,0:T(8,128)(2,1)} %param.11), channel_id=1, source_target_pairs={{0,1},{1,2},{2,3},{3,4},{4,5},{5,6},{6,7},{7,8},{8,9},{9,10},{10,1... | collective-permute-start | bytes 2359304 | tf_op jit(solution)/shard_map/ppermute | solution.py:15
  21.3 130.3 %collective-permute-start.2 = (bf16[16,16,1536]{2,1,0:T(8,128)(2,1)}, bf16[16,16,1536]{2,1,0:T(8,128)(2,1)S(1)}, u32[]{:S(2)}, u32[]{:S(2)}) collective-permute-start(bf16[16,16,1536]{2,1,0:T(8,128)(2,1)} %param.10), channel_id=1, source_target_pairs={{0,63},{1,0},{2,1},{3,2},{4,3},{5,4},{6,5},{7,6},{8,7},{9,8},{10,9... | collective-permute-start | bytes 2359304 | tf_op jit(solution)/shard_map/ppermute | solution.py:15
  24.4 125.2 %collective-permute-start.1 = (bf16[16,16,1536]{2,1,0:T(8,128)(2,1)}, bf16[16,16,1536]{2,1,0:T(8,128)(2,1)S(1)}, u32[]{:S(2)}, u32[]{:S(2)}) collective-permute-start(bf16[16,16,1536]{2,1,0:T(8,128)(2,1)} %param.10), channel_id=1, source_target_pairs={{0,1},{1,2},{2,3},{3,4},{4,5},{5,6},{6,7},{7,8},{8,9},{9,10},{10,1... | collective-permute-start | bytes 2359304 | tf_op jit(solution)/shard_map/ppermute | solution.py:15
  44.9 68.9 %collective-permute-start.6 = (bf16[16,16,1536]{2,1,0:T(8,128)(2,1)}, bf16[16,16,1536]{2,1,0:T(8,128)(2,1)S(1)}, u32[]{:S(2)}, u32[]{:S(2)}) collective-permute-start(bf16[16,16,1536]{2,1,0:T(8,128)(2,1)} %param.11), channel_id=1, source_target_pairs={{0,63},{1,0},{2,1},{3,2},{4,3},{5,4},{6,5},{7,6},{8,7},{9,8},{10,9... | collective-permute-start | bytes 2359304 | tf_op jit(solution)/shard_map/ppermute | solution.py:15
  80.9 67.7 %collective-permute-start.7 = (bf16[16,16,1536]{2,1,0:T(8,128)(2,1)}, bf16[16,16,1536]{2,1,0:T(8,128)(2,1)S(1)}, u32[]{:S(2)}, u32[]{:S(2)}) collective-permute-start(bf16[16,16,1536]{2,1,0:T(8,128)(2,1)} %param.11), channel_id=1, source_target_pairs={{0,62},{1,63},{2,0},{3,1},{4,2},{5,3},{6,4},{7,5},{8,6},{9,7},{10,... | collective-permute-start | bytes 2359304 | tf_op jit(solution)/shard_map/ppermute | solution.py:15
  108.0 59.4 %collective-permute-start.3 = (bf16[16,16,1536]{2,1,0:T(8,128)(2,1)S(1)}, bf16[16,16,1536]{2,1,0:T(8,128)(2,1)S(1)}, u32[]{:S(2)}, u32[]{:S(2)}) collective-permute-start(bf16[16,16,1536]{2,1,0:T(8,128)(2,1)S(1)} %copy-done.8), channel_id=1, source_target_pairs={{0,62},{1,63},{2,0},{3,1},{4,2},{5,3},{6,4},{7,5},{8,6},{9,7},{10,... | collective-permute-start | bytes 2359304 | tf_op jit(solution)/shard_map/ppermute | solution.py:15
  199.5 125.8 %copy-start.9 = (s32[2,1,8]{2,1,0:T(1,128)S(1)}, s32[2,1,8]{2,1,0:T(1,128)}, u32[]{:S(2)}) copy-start(s32[2,1,8]{2,1,0:T(1,128)} %param.12) | copy-start | bytes 196
  348.2 6.0 %copy-start.2 = (bf16[1024,24,64]{0,2,1:T(8,128)(2,1)S(1)}, bf16[1024,24,64]{0,2,1:T(8,128)(2,1)}, u32[]{:S(2)}) copy-start(bf16[1024,24,64]{0,2,1:T(8,128)(2,1)} %concatenate.17) | copy-start | bytes 9437188 | tf_op jit(solution)/shard_map/conditional.1
  366.1 11.7 %copy-start.4 = (bf16[1024,24,64]{0,2,1:T(8,128)(2,1)S(1)}, bf16[1024,24,64]{0,2,1:T(8,128)(2,1)}, u32[]{:S(2)}) copy-start(bf16[1024,24,64]{0,2,1:T(8,128)(2,1)} %concatenate.2) | copy-start | bytes 9437188 | tf_op jit(solution)/shard_map/conditional.1
  366.1 11.7 %copy-start.6 = (bf16[1024,1536]{0,1:T(8,128)(2,1)S(1)}, bf16[1024,1536]{0,1:T(8,128)(2,1)}, u32[]{:S(2)}) copy-start(bf16[1024,1536]{0,1:T(8,128)(2,1)} %get-tuple-element.72) | copy-start | bytes 9437188 | tf_op jit(solution)/shard_map/conditional.1
  389.3 0.8 copy-start.5
  414.9 6.0 %copy-start.2 = (bf16[1024,24,64]{0,2,1:T(8,128)(2,1)S(1)}, bf16[1024,24,64]{0,2,1:T(8,128)(2,1)}, u32[]{:S(2)}) copy-start(bf16[1024,24,64]{0,2,1:T(8,128)(2,1)} %concatenate.17) | copy-start | bytes 9437188 | tf_op jit(solution)/shard_map/conditional.1
  432.7 11.7 %copy-start.4 = (bf16[1024,24,64]{0,2,1:T(8,128)(2,1)S(1)}, bf16[1024,24,64]{0,2,1:T(8,128)(2,1)}, u32[]{:S(2)}) copy-start(bf16[1024,24,64]{0,2,1:T(8,128)(2,1)} %concatenate.2) | copy-start | bytes 9437188 | tf_op jit(solution)/shard_map/conditional.1
  432.7 11.7 %copy-start.6 = (bf16[1024,1536]{0,1:T(8,128)(2,1)S(1)}, bf16[1024,1536]{0,1:T(8,128)(2,1)}, u32[]{:S(2)}) copy-start(bf16[1024,1536]{0,1:T(8,128)(2,1)} %get-tuple-element.72) | copy-start | bytes 9437188 | tf_op jit(solution)/shard_map/conditional.1
  455.9 0.8 copy-start.5
Sparse Core Ops, SparseCore 0:
  11.0 183.7 all-gather.6
  198.5 122.1 all-gather.4
where the time goes:
time: 467 us; the launch traced here: 465 us
  waiting for transfers between devices  235 us (50%)
  local copies, waits for them, and re-layouts  90.3 us (19%)
  starting transfers between devices  55.8 us (12%)
  matrix products  46.7 us (10%)
  other arithmetic  24.1 us (5%)
  between operations  13.4 us (3%)
    all_gather x1, waiting for transfers between devices, local(): lax.all_gather(picked_values, 'lon', axis=0, tiled=True)  121 us
    ppermute x8, waiting for transfers between devices, from_behind(): return lax.ppermute(value, axis, pairs)  87.2 us
    ppermute x8, starting transfers between devices, from_behind(): return lax.ppermute(value, axis, pairs)  55.7 us
    all_gather x1, waiting for transfers between devices, local(): lax.all_gather(picked_keys, 'lon', axis=0, tiled=True)  26.5 us
    dot_general x2, matrix products, block_attention(): jnp.einsum('qhd,khd->hqk', q_heads, k_heads, preferred_element_type=jnp.f...  23.7 us
    reduce_sum x2, other arithmetic, block_attention(): totals = jnp.sum(exp_scores, axis=-1)  23.3 us
    dot_general x2, matrix products, block_attention(): jnp.einsum('hqk,khd->qhd', weights, v_heads, preferred_element_type=jnp.f...  23 us
    another operation x16, local copies, waits for them, and re-layouts  16.8 us
  transfers between devices with their start and end apart: 10, of which 7 were waited for; matrix products, arithmetic and copies ran while one was open for 4% of the time, Pallas kernels for 0%

commit v1 on v0

--- a/solution.py
+++ b/solution.py
@@ -53,7 +53,9 @@
     picked_values = value_tokens.reshape(tile_lat * tile_lon, feature)[band_rows[0]]
     band_keys, band_values = (
         lax.all_gather(picked_keys, "lon", axis=0, tiled=True),
-        lax.all_gather(picked_values, "lon", axis=0, tiled=True),
+        jnp.concatenate(
+            lax.all_to_all(jnp.stack([picked_values] * lax.axis_size("lon")), "lon", 0, 0), axis=0
+        ),
     )
     lat_at = lax.axis_index("lat")
     is_polar = (lat_at == 0) | (lat_at == lat_size - 1)

time: 467 us -> 396 us (0.85)
  waiting for transfers between devices: 235 us -> 164 us
  starting transfers between devices: 55.8 us -> 49.6 us
    all_gather x1 -> x0, waiting for transfers between devices: 121 us -> none  [local(): lax.all_gather(picked_values, 'lon', axis=0, tiled=True)]
    ppermute x8, waiting for transfers between devices: 87.2 us -> 164 us  [from_behind(): return lax.ppermute(value, axis, pairs)]
    all_gather x1, waiting for transfers between devices: 26.5 us -> 0.01 us  [local(): lax.all_gather(picked_keys, 'lon', axis=0, tiled=True)]
    ppermute x8, starting transfers between devices: 55.7 us -> 35 us  [from_behind(): return lax.ppermute(value, axis, pairs)]
    all_to_all x0 -> x1, starting transfers between devices: none -> 14.6 us  [local(): lax.all_to_all(jnp.stack([picked_values] * lax.axis_size('lon')), 'lon',...]
    another operation x16 -> x17, local copies, waits for them, and re-layouts: 16.8 us -> 18.9 us
  transfers between devices with their start and end apart: 10 -> 10, of which waited for: 7 -> 5; matrix products, arithmetic and copies ran while one was open for 4% -> 5% of each run, Pallas kernels for 0% -> 0%
where the time goes in v1:
time: 396 us; the launch traced here: 390 us
  waiting for transfers between devices  164 us (41%)
  local copies, waits for them, and re-layouts  92.3 us (23%)
  starting transfers between devices  49.6 us (13%)
  matrix products  46.7 us (12%)
  other arithmetic  24 us (6%)
  between operations  13.4 us (3%)
    ppermute x8, waiting for transfers between devices, from_behind(): return lax.ppermute(value, axis, pairs)  164 us
    ppermute x8, starting transfers between devices, from_behind(): return lax.ppermute(value, axis, pairs)  35 us
    dot_general x2, matrix products, block_attention(): jnp.einsum('qhd,khd->hqk', q_heads, k_heads, preferred_element_type=jnp.f...  23.7 us
    reduce_sum x2, other arithmetic, block_attention(): totals = jnp.sum(exp_scores, axis=-1)  23.3 us
    dot_general x2, matrix products, block_attention(): jnp.einsum('hqk,khd->qhd', weights, v_heads, preferred_element_type=jnp.f...  23 us
    another operation x16, local copies, waits for them, and re-layouts  16.8 us
    all_to_all x1, starting transfers between devices, local(): lax.all_to_all(jnp.stack([picked_values] * lax.axis_size('lon')), 'lon',...  14.6 us
    unnamed x14, local copies, waits for them, and re-layouts  13.4 us
  transfers between devices with their start and end apart: 10, of which 5 were waited for; matrix products, arithmetic and copies ran while one was open for 5% of the time, Pallas kernels for 0%

profile of v1, /device:TPU:8, one launch (start us, length us, event | category | flops | bytes accessed | tf_op | source)
XLA Modules:
  0.0 390.4 jit_solution(7236557583487858519)
XLA Ops:
  11.1 14.6 %all-to-all-start = ((bf16[64,16,1536]{2,1,0:T(8,128)(2,1)}), bf16[64,16,1536]{2,1,0:T(8,128)(2,1)S(1)}, u32[]{:S(2)}, u32[]{:S(2)}) async-start(bf16[64,16,1536]{2,1,0:T(8,128)(2,1)} %stack.2), calls=%async_computation | async-start | bytes 6291456 | tf_op jit(solution)/shard_map/all_to_all | solution.py:57
  30.7 3.6 collective-permute-start
  34.9 3.6 collective-permute-start.2
  38.4 94.1 %collective-permute-done.4 = bf16[16,16,1536]{2,1,0:T(8,128)(2,1)} collective-permute-done((bf16[16,16,1536]{2,1,0:T(8,128)(2,1)}, bf16[16,16,1536]{2,1,0:T(8,128)(2,1)}, u32[]{:S(2)}, u32[]{:S(2)}) %collective-permute-start.4) | collective-permute-done | bytes 786464 | tf_op jit(solution)/shard_map/ppermute | solution.py:15
  132.5 19.5 %collective-permute-start.6 = (bf16[16,16,1536]{2,1,0:T(8,128)(2,1)}, bf16[16,16,1536]{2,1,0:T(8,128)(2,1)S(1)}, u32[]{:S(2)}, u32[]{:S(2)}) collective-permute-start(bf16[16,16,1536]{2,1,0:T(8,128)(2,1)} %param.11), channel_id=1, source_target_pairs={{0,63},{1,0},{2,1},{3,2},{4,3},{5,4},{6,5},{7,6},{8,7},{9,8},{10,9... | collective-permute-start | bytes 2359304 | tf_op jit(solution)/shard_map/ppermute | solution.py:15
  154.1 26.2 %collective-permute-done = bf16[16,16,1536]{2,1,0:T(8,128)(2,1)} collective-permute-done((bf16[16,16,1536]{2,1,0:T(8,128)(2,1)}, bf16[16,16,1536]{2,1,0:T(8,128)(2,1)}, u32[]{:S(2)}, u32[]{:S(2)}) %collective-permute-start) | collective-permute-done | bytes 786464 | tf_op jit(solution)/shard_map/ppermute | solution.py:15
  180.3 3.0 collective-permute-start.7
  185.4 11.8 %collective-permute-done.5 = bf16[16,16,1536]{2,1,0:T(8,128)(2,1)} collective-permute-done((bf16[16,16,1536]{2,1,0:T(8,128)(2,1)}, bf16[16,16,1536]{2,1,0:T(8,128)(2,1)}, u32[]{:S(2)}, u32[]{:S(2)}) %collective-permute-start.5) | collective-permute-done | bytes 786464 | tf_op jit(solution)/shard_map/ppermute | solution.py:15
  203.6 29.6 %collective-permute-done.7 = bf16[16,16,1536]{2,1,0:T(8,128)(2,1)S(1)} collective-permute-done((bf16[16,16,1536]{2,1,0:T(8,128)(2,1)}, bf16[16,16,1536]{2,1,0:T(8,128)(2,1)S(1)}, u32[]{:S(2)}, u32[]{:S(2)}) %collective-permute-start.7) | collective-permute-done | bytes 786464 | tf_op jit(solution)/shard_map/ppermute | solution.py:15
  242.8 2.9 copy.16
  245.7 4.6 %copy.17 = bf16[1024,1536]{0,1:T(8,128)(2,1)} copy(bf16[1024,1536]{1,0:T(8,128)(2,1)} %all-gather.3.cloned.1.call-done) | data formatting | bytes 6291456 | tf_op jit(solution)/shard_map/while | solution.py:83
  250.3 133.3 %while.10 = (s32[]{:T(128)}, bf16[2,128,1536]{2,1,0:T(8,128)(2,1)}, pred[]{:T(512)}, bf16[2,128,1536]{2,1,0:T(8,128)(2,1)}, s32[2,8]{1,0:T(2,128)S(1)}, /*index=...) while((s32[]{:T(128)}, bf16[2,128,1536]{2,1,0:T(8,128)(2,1)}, ...), condition=%wide.region_7.8_spmd, body=%wide.region_0.7_spmd.sunk | while | flops 1686498304 | bytes 169148896 | solution.py:83
  251.6 2.9 gather_fusion.1
  254.5 4.5 %gather_fusion = bf16[8,128,1536]{2,1,0:T(8,128)(2,1)} fusion(bf16[10,128,1536]{2,1,0:T(8,128)(2,1)} %get-tuple-element.216, s32[1024]{0:T(1024)S(1)} %pad_clamp_fusion.3), kind=kCustom, calls=%fused_computation.clone.1 | custom fusion | bytes 6291488 | tf_op jit(solution)/shard_map/while/body/eval_jaxpr/gather | solution.py:68
  259.0 55.2 %conditional.7 = (bf16[1,128,1536]{1,2,0:T(8,128)(2,1)S(1)}) conditional(s32[]{:T(128)} %convert_element_type.36, (bf16[128,1536]{0,1:T(8,128)(2,1)S(1)}, bf16[8,128,1536]{2,1,0:T(8,128)(2,1)}, bf16[8,128,1536]{2,1,0:T(8,128)(2,1)S(1)}) %tuple.51, (bf16[8,128,1536]{2,1,0:T(8,128)(2,1)S(1)}, bf16[1024,1536]{0,1:T(8,128)(2,1)}, ...), branch_computations={%region_1.3_spmd, %region_4.6_spmd} | conditional | flops 1686497280 | bytes 151842912
  259.0 5.0 %copy.14 = bf16[8,128,1536]{1,0,2:T(8,128)(2,1)} copy(bf16[8,128,1536]{2,1,0:T(8,128)(2,1)} %get-tuple-element.102) | data formatting | bytes 6291456 | tf_op jit(solution)/shard_map
  264.0 5.8 %concatenate.17 = bf16[1024,24,64]{0,2,1:T(8,128)(2,1)} reshape(bf16[8,128,1536]{1,0,2:T(8,128)(2,1)} %copy.14) | data formatting | bytes 6291456 | tf_op jit(solution)/shard_map/while/body/eval_jaxpr/cond/branch_1_fun/concatenate | solution.py:73
  269.8 3.4 copy.13
  273.2 6.0 %concatenate.2 = bf16[1024,24,64]{0,2,1:T(8,128)(2,1)} reshape(bf16[8,128,1536]{1,0,2:T(8,128)(2,1)} %copy.13) | data formatting | bytes 6291456 | tf_op jit(solution)/shard_map/while/body/eval_jaxpr/cond/branch_1_fun/concatenate | solution.py:74
  279.2 11.8 %bitcast_reduce_fusion = (f32[24,128]{1,0:T(8,128)S(1)}, f32[24,2048,128]{2,1,0:T(8,128)}) fusion(bf16[128,24,64]{0,2,1:T(8,128)(2,1)S(1)} %bitcast.101, bf16[1024,24,64]{0,2,1:T(8,128)(2,1)} %bitcast.97, bf16[1024,24,64]{0,2,1:T(8,128)(2,1)S(1)} %copy-done.2), kind=kOutput, calls=%fused_computation.15 | convolution fusion | flops 830469120 | bytes 31862784 | tf_op jit(solution)/shard_map/while/body/eval_jaxpr/cond/branch_1_fun/qhd,khd->hqk/dot_general | solution.py:23
  291.0 11.7 %fusion.14 = f32[24,128]{1,0:T(8,128)S(1)} fusion(f32[24,2048,128]{2,1,0:T(8,128)} %get-tuple-element.135, f32[24,128]{1,0:T(8,128)S(1)} %get-tuple-element.134), kind=kLoop, calls=%fused_computation.17 | loop fusion | flops 18871296 | bytes 25190400 | tf_op jit(solution)/shard_map/while/body/eval_jaxpr/cond/branch_1_fun/reduce_sum | solution.py:29
  302.7 11.5 %fusion.32 = bf16[128,24,64]{0,2,1:T(8,128)(2,1)S(1)} fusion(f32[24,2048,128]{2,1,0:T(8,128)} %get-tuple-element.135, f32[24,128]{1,0:T(8,128)S(1)} %get-tuple-element.134, bf16[1024,24,64]{0,2,1:T(8,128)(2,1)S(1)} %bitcast.105, bf16[1024,24,64]{0,2,1:T(8,128)(2,1)S(1)} %copy-done.4, f32[128,24]{0,1:T(8,128)S(1)} %bitcast.113), kind=kOutput, calls=%fused_computation.30 | convolution fusion | flops 837156864 | bytes 31875072 | tf_op jit(solution)/shard_map/while/body/eval_jaxpr/cond/branch_1_fun/hqk,khd->qhd/dot_general | solution.py:31
  318.2 2.9 gather_fusion.1
  321.1 4.5 %gather_fusion = bf16[8,128,1536]{2,1,0:T(8,128)(2,1)} fusion(bf16[10,128,1536]{2,1,0:T(8,128)(2,1)} %get-tuple-element.216, s32[1024]{0:T(1024)S(1)} %pad_clamp_fusion.3), kind=kCustom, calls=%fused_computation.clone.1 | custom fusion | bytes 6291488 | tf_op jit(solution)/shard_map/while/body/eval_jaxpr/gather | solution.py:68
  325.6 55.2 %conditional.7 = (bf16[1,128,1536]{1,2,0:T(8,128)(2,1)S(1)}) conditional(s32[]{:T(128)} %convert_element_type.36, (bf16[128,1536]{0,1:T(8,128)(2,1)S(1)}, bf16[8,128,1536]{2,1,0:T(8,128)(2,1)}, bf16[8,128,1536]{2,1,0:T(8,128)(2,1)S(1)}) %tuple.51, (bf16[8,128,1536]{2,1,0:T(8,128)(2,1)S(1)}, bf16[1024,1536]{0,1:T(8,128)(2,1)}, ...), branch_computations={%region_1.3_spmd, %region_4.6_spmd} | conditional | flops 1686497280 | bytes 151842912
  325.6 5.0 %copy.14 = bf16[8,128,1536]{1,0,2:T(8,128)(2,1)} copy(bf16[8,128,1536]{2,1,0:T(8,128)(2,1)} %get-tuple-element.102) | data formatting | bytes 6291456 | tf_op jit(solution)/shard_map
  330.6 5.8 %concatenate.17 = bf16[1024,24,64]{0,2,1:T(8,128)(2,1)} reshape(bf16[8,128,1536]{1,0,2:T(8,128)(2,1)} %copy.14) | data formatting | bytes 6291456 | tf_op jit(solution)/shard_map/while/body/eval_jaxpr/cond/branch_1_fun/concatenate | solution.py:73
  336.4 3.4 copy.13
  339.8 6.0 %concatenate.2 = bf16[1024,24,64]{0,2,1:T(8,128)(2,1)} reshape(bf16[8,128,1536]{1,0,2:T(8,128)(2,1)} %copy.13) | data formatting | bytes 6291456 | tf_op jit(solution)/shard_map/while/body/eval_jaxpr/cond/branch_1_fun/concatenate | solution.py:74
  345.8 11.8 %bitcast_reduce_fusion = (f32[24,128]{1,0:T(8,128)S(1)}, f32[24,2048,128]{2,1,0:T(8,128)}) fusion(bf16[128,24,64]{0,2,1:T(8,128)(2,1)S(1)} %bitcast.101, bf16[1024,24,64]{0,2,1:T(8,128)(2,1)} %bitcast.97, bf16[1024,24,64]{0,2,1:T(8,128)(2,1)S(1)} %copy-done.2), kind=kOutput, calls=%fused_computation.15 | convolution fusion | flops 830469120 | bytes 31862784 | tf_op jit(solution)/shard_map/while/body/eval_jaxpr/cond/branch_1_fun/qhd,khd->hqk/dot_general | solution.py:23
  357.7 11.7 %fusion.14 = f32[24,128]{1,0:T(8,128)S(1)} fusion(f32[24,2048,128]{2,1,0:T(8,128)} %get-tuple-element.135, f32[24,128]{1,0:T(8,128)S(1)} %get-tuple-element.134), kind=kLoop, calls=%fused_computation.17 | loop fusion | flops 18871296 | bytes 25190400 | tf_op jit(solution)/shard_map/while/body/eval_jaxpr/cond/branch_1_fun/reduce_sum | solution.py:29
  369.4 11.5 %fusion.32 = bf16[128,24,64]{0,2,1:T(8,128)(2,1)S(1)} fusion(f32[24,2048,128]{2,1,0:T(8,128)} %get-tuple-element.135, f32[24,128]{1,0:T(8,128)S(1)} %get-tuple-element.134, bf16[1024,24,64]{0,2,1:T(8,128)(2,1)S(1)} %bitcast.105, bf16[1024,24,64]{0,2,1:T(8,128)(2,1)S(1)} %copy-done.4, f32[128,24]{0,1:T(8,128)S(1)} %bitcast.113), kind=kOutput, calls=%fused_computation.30 | convolution fusion | flops 837156864 | bytes 31875072 | tf_op jit(solution)/shard_map/while/body/eval_jaxpr/cond/branch_1_fun/hqk,khd->qhd/dot_general | solution.py:31
  (62 shorter events, 38.4 us)
Async XLA Ops:
  11.1 231.6 %all-to-all-start = ((bf16[64,16,1536]{2,1,0:T(8,128)(2,1)}), bf16[64,16,1536]{2,1,0:T(8,128)(2,1)S(1)}, u32[]{:S(2)}, u32[]{:S(2)}) async-start(bf16[64,16,1536]{2,1,0:T(8,128)(2,1)} %stack.2), calls=%async_computation | async-start | bytes 6291456 | tf_op jit(solution)/shard_map/all_to_all | solution.py:57
  25.7 219.9 %all-gather.3.cloned.1.call-start = ((), (), s32[]{:S(2)}) async-start(), calls=%async_computation.1 | async-start | bytes 3194880 | tf_op jit(solution)/shard_map/all_gather | solution.py:55
  28.3 104.2 %collective-permute-start.4 = (bf16[16,16,1536]{2,1,0:T(8,128)(2,1)}, bf16[16,16,1536]{2,1,0:T(8,128)(2,1)}, u32[]{:S(2)}, u32[]{:S(2)}) collective-permute-start(bf16[16,16,1536]{2,1,0:T(8,128)(2,1)} %param.11), channel_id=1, source_target_pairs={{0,2},{1,3},{2,4},{3,5},{4,6},{5,7},{6,8},{7,9},{8,10},{9,11},{10,... | collective-permute-start | bytes 2359304 | tf_op jit(solution)/shard_map/ppermute | solution.py:15
  30.7 149.6 %collective-permute-start = (bf16[16,16,1536]{2,1,0:T(8,128)(2,1)}, bf16[16,16,1536]{2,1,0:T(8,128)(2,1)}, u32[]{:S(2)}, u32[]{:S(2)}) collective-permute-start(bf16[16,16,1536]{2,1,0:T(8,128)(2,1)} %param.10), channel_id=1, source_target_pairs={{0,2},{1,3},{2,4},{3,5},{4,6},{5,7},{6,8},{7,9},{8,10},{9,11},{10,... | collective-permute-start | bytes 2359304 | tf_op jit(solution)/shard_map/ppermute | solution.py:15
  34.3 162.9 %collective-permute-start.5 = (bf16[16,16,1536]{2,1,0:T(8,128)(2,1)}, bf16[16,16,1536]{2,1,0:T(8,128)(2,1)}, u32[]{:S(2)}, u32[]{:S(2)}) collective-permute-start(bf16[16,16,1536]{2,1,0:T(8,128)(2,1)} %param.11), channel_id=1, source_target_pairs={{0,1},{1,2},{2,3},{3,4},{4,5},{5,6},{6,7},{7,8},{8,9},{9,10},{10,1... | collective-permute-start | bytes 2359304 | tf_op jit(solution)/shard_map/ppermute | solution.py:15
  34.9 202.3 %collective-permute-start.2 = (bf16[16,16,1536]{2,1,0:T(8,128)(2,1)}, bf16[16,16,1536]{2,1,0:T(8,128)(2,1)}, u32[]{:S(2)}, u32[]{:S(2)}) collective-permute-start(bf16[16,16,1536]{2,1,0:T(8,128)(2,1)} %param.10), channel_id=1, source_target_pairs={{0,63},{1,0},{2,1},{3,2},{4,3},{5,4},{6,5},{7,6},{8,7},{9,8},{10,9... | collective-permute-start | bytes 2359304 | tf_op jit(solution)/shard_map/ppermute | solution.py:15
  38.4 195.7 %collective-permute-start.1 = (bf16[16,16,1536]{2,1,0:T(8,128)(2,1)}, bf16[16,16,1536]{2,1,0:T(8,128)(2,1)}, u32[]{:S(2)}, u32[]{:S(2)}) collective-permute-start(bf16[16,16,1536]{2,1,0:T(8,128)(2,1)} %param.10), channel_id=1, source_target_pairs={{0,1},{1,2},{2,3},{3,4},{4,5},{5,6},{6,7},{7,8},{8,9},{9,10},{10,1... | collective-permute-start | bytes 2359304 | tf_op jit(solution)/shard_map/ppermute | solution.py:15
  38.4 163.3 %copy-start.7 = (bf16[16,16,1536]{2,1,0:T(8,128)(2,1)S(1)}, bf16[16,16,1536]{2,1,0:T(8,128)(2,1)}, u32[]{:S(2)}) copy-start(bf16[16,16,1536]{2,1,0:T(8,128)(2,1)} %param.11) | copy-start | bytes 2359300
  132.5 70.1 %collective-permute-start.6 = (bf16[16,16,1536]{2,1,0:T(8,128)(2,1)}, bf16[16,16,1536]{2,1,0:T(8,128)(2,1)S(1)}, u32[]{:S(2)}, u32[]{:S(2)}) collective-permute-start(bf16[16,16,1536]{2,1,0:T(8,128)(2,1)} %param.11), channel_id=1, source_target_pairs={{0,63},{1,0},{2,1},{3,2},{4,3},{5,4},{6,5},{7,6},{8,7},{9,8},{10,9... | collective-permute-start | bytes 2359304 | tf_op jit(solution)/shard_map/ppermute | solution.py:15
  180.3 52.9 %collective-permute-start.7 = (bf16[16,16,1536]{2,1,0:T(8,128)(2,1)}, bf16[16,16,1536]{2,1,0:T(8,128)(2,1)S(1)}, u32[]{:S(2)}, u32[]{:S(2)}) collective-permute-start(bf16[16,16,1536]{2,1,0:T(8,128)(2,1)} %param.11), channel_id=1, source_target_pairs={{0,62},{1,63},{2,0},{3,1},{4,2},{5,3},{6,4},{7,5},{8,6},{9,7},{10,... | collective-permute-start | bytes 2359304 | tf_op jit(solution)/shard_map/ppermute | solution.py:15
  197.2 44.7 %collective-permute-start.3 = (bf16[16,16,1536]{2,1,0:T(8,128)(2,1)}, bf16[16,16,1536]{2,1,0:T(8,128)(2,1)S(1)}, u32[]{:S(2)}, u32[]{:S(2)}) collective-permute-start(bf16[16,16,1536]{2,1,0:T(8,128)(2,1)} %param.10), channel_id=1, source_target_pairs={{0,62},{1,63},{2,0},{3,1},{4,2},{5,3},{6,4},{7,5},{8,6},{9,7},{10,... | collective-permute-start | bytes 2359304 | tf_op jit(solution)/shard_map/ppermute | solution.py:15
  199.6 36.6 %copy-start.8 = (bf16[16,16,1536]{2,1,0:T(8,128)(2,1)S(1)}, bf16[16,16,1536]{2,1,0:T(8,128)(2,1)}, u32[]{:S(2)}) copy-start(bf16[16,16,1536]{2,1,0:T(8,128)(2,1)} %param.10) | copy-start | bytes 2359300
  245.7 4.6 %copy-start.9 = (s32[2,1,8]{2,1,0:T(1,128)S(1)}, s32[2,1,8]{2,1,0:T(1,128)}, u32[]{:S(2)}) copy-start(s32[2,1,8]{2,1,0:T(1,128)} %param.12) | copy-start | bytes 196
  273.2 6.0 %copy-start.2 = (bf16[1024,24,64]{0,2,1:T(8,128)(2,1)S(1)}, bf16[1024,24,64]{0,2,1:T(8,128)(2,1)}, u32[]{:S(2)}) copy-start(bf16[1024,24,64]{0,2,1:T(8,128)(2,1)} %concatenate.17) | copy-start | bytes 9437188 | tf_op jit(solution)/shard_map/conditional.1
  291.0 11.7 %copy-start.4 = (bf16[1024,24,64]{0,2,1:T(8,128)(2,1)S(1)}, bf16[1024,24,64]{0,2,1:T(8,128)(2,1)}, u32[]{:S(2)}) copy-start(bf16[1024,24,64]{0,2,1:T(8,128)(2,1)} %concatenate.2) | copy-start | bytes 9437188 | tf_op jit(solution)/shard_map/conditional.1
  291.0 11.7 %copy-start.6 = (bf16[1024,1536]{0,1:T(8,128)(2,1)S(1)}, bf16[1024,1536]{0,1:T(8,128)(2,1)}, u32[]{:S(2)}) copy-start(bf16[1024,1536]{0,1:T(8,128)(2,1)} %get-tuple-element.72) | copy-start | bytes 9437188 | tf_op jit(solution)/shard_map/conditional.1
  314.2 0.8 copy-start.5
  339.8 6.0 %copy-start.2 = (bf16[1024,24,64]{0,2,1:T(8,128)(2,1)S(1)}, bf16[1024,24,64]{0,2,1:T(8,128)(2,1)}, u32[]{:S(2)}) copy-start(bf16[1024,24,64]{0,2,1:T(8,128)(2,1)} %concatenate.17) | copy-start | bytes 9437188 | tf_op jit(solution)/shard_map/conditional.1
  357.7 11.7 %copy-start.4 = (bf16[1024,24,64]{0,2,1:T(8,128)(2,1)S(1)}, bf16[1024,24,64]{0,2,1:T(8,128)(2,1)}, u32[]{:S(2)}) copy-start(bf16[1024,24,64]{0,2,1:T(8,128)(2,1)} %concatenate.2) | copy-start | bytes 9437188 | tf_op jit(solution)/shard_map/conditional.1
  357.7 11.7 %copy-start.6 = (bf16[1024,1536]{0,1:T(8,128)(2,1)S(1)}, bf16[1024,1536]{0,1:T(8,128)(2,1)}, u32[]{:S(2)}) copy-start(bf16[1024,1536]{0,1:T(8,128)(2,1)} %get-tuple-element.72) | copy-start | bytes 9437188 | tf_op jit(solution)/shard_map/conditional.1
  380.9 0.8 copy-start.5
Sparse Core Ops, SparseCore 0:
  30.2 141.0 all-gather.2
